TPU v7x, 32 devices: a whole 2x2x4 slice. The times are simulated.
32 devices in a mesh: ma: 8 (over z, core), row: 4 (over y, x).
Axes of the slice: x: 2, y: 2, z: 4, core: 2. Of those that a mesh axis runs over, the one named last changes fastest.
Arguments:
- seed_field: bfloat16 [4, 4, 2, 1024, 1024], P(None, 'row', None, 'ma'), may hold values from -6 to 6
- cotangent: bfloat16 [2, 4, 2, 1024, 1024], P(None, 'row', None, 'ma'), may hold values from -6 to 6
- step_size: float32 [1], replicated, may hold values from 0.25 to 1
- owner_list: int32 [1024], replicated, may hold values from 0 to 1023, as said below
Outputs:
- nonlinear: float32 [2, 4, 2, 1024, 1024], P(None, 'row', None, 'ma')
- seed_next: float32 [4, 4, 2, 1024, 1024], P(None, 'row', None, 'ma')
Inputs may be any that keep to these rules, and one draw needn't show every extreme that they name: owner_list is a permutation of the wavenumbers; entries 128 d to 128 (d + 1) - 1 name the wavenumbers of owner d, and a block that holds m also holds 1023 - m.
All inputs are finite; a program needn't handle non-finite values.
Results may differ from a plain program's by a relative error of at most 0.0082.
Values may be sent and summed in bfloat16 or wider, within the bound.
No kernel may reach another device: no remote copies, remote signals or barrier semaphores. Data moves between devices by JAX's collectives and lax.ppermute only.
A program may use at most 128 MiB of HBM per device.

v0:
```python
import math

import jax
import jax.numpy as jnp
from jax import lax
from jax.sharding import PartitionSpec as P

WAVES = 1024
DEGREES = 1024
NLAT = 1024
NLON = 2048


def lat_cosines(theta_index):
    degree = jnp.arange(DEGREES, dtype=jnp.int32)
    phase_index = (2 * theta_index[:, None] + 1) * degree[None, :] % (4 * NLAT)
    return jnp.cos(phase_index.astype(jnp.float32) * (math.pi / (2 * NLAT))).astype(jnp.bfloat16)


def wave_cosines(wave_ids):
    points = jnp.arange(NLON, dtype=jnp.int32)
    phase_index = wave_ids[:, None] * points[None, :] % NLON
    angles = phase_index.astype(jnp.float32) * (2.0 * math.pi / NLON)
    return jnp.stack([jnp.cos(angles), -jnp.sin(angles)]).astype(jnp.bfloat16)


def local(seed_field, cotangent, step_size, owner_list):
    owner_count = lax.axis_size("ma")
    own_waves = cotangent.shape[3]
    norm_scale = 2.0 / math.sqrt(DEGREES * WAVES)
    block_width = min(128, WAVES)
    my_waves = lax.dynamic_slice_in_dim(owner_list, lax.axis_index("ma") * own_waves, own_waves)
    degree = jnp.arange(DEGREES, dtype=jnp.int32)
    live_cols = degree[:, None] >= my_waves[None, :]
    live_rows = jnp.transpose(live_cols)
    zero_value = jnp.zeros((), jnp.bfloat16)
    listed = jnp.take(seed_field, owner_list, axis=4)
    owned_seed = lax.all_to_all(listed, "ma", split_axis=4, concat_axis=3, tiled=True)
    lat_table = lat_cosines(jnp.arange(NLAT, dtype=jnp.int32))
    forward_rows = jnp.einsum(
        "crslk,tl->crstk",
        jnp.where(live_cols, owned_seed, zero_value),
        lat_table,
        preferred_element_type=jnp.float32,
    )
    adjoint_rows = jnp.einsum(
        "crskl,tl->crstk",
        jnp.where(live_rows, cotangent, zero_value),
        lat_table,
        preferred_element_type=jnp.float32,
    )
    spec_rows = jnp.concatenate([forward_rows, adjoint_rows], axis=0).astype(jnp.bfloat16)
    gridded = lax.all_to_all(
        lax.all_to_all(spec_rows, "ma", split_axis=3, concat_axis=4, tiled=True),
        "row",
        split_axis=3,
        concat_axis=1,
        tiled=True,
    )
    grid_field = None
    for start in range(0, WAVES, block_width):
        wave_block = wave_cosines(owner_list[start : start + block_width])
        partial_grid = jnp.einsum(
            "crsjm,smf->crjf",
            gridded[..., start : start + block_width],
            wave_block,
            preferred_element_type=jnp.float32,
        )
        grid_field = partial_grid if grid_field is None else grid_field + partial_grid
    grid_field = norm_scale * grid_field
    radial_pair = jnp.stack([grid_field[1], grid_field[3]])
    padded = jnp.pad(radial_pair, ((0, 0), (1, 1), (0, 0), (0, 0)))
    slopes = 0.5 * (padded[:, 2:] - padded[:, :-2])
    vel_tor = grid_field[0]
    mag_tor = grid_field[2]
    adj_vel = grid_field[4]
    adj_mag = grid_field[5]
    vel_pol = slopes[0]
    mag_pol = slopes[1]
    term_vel = mag_tor * mag_pol - vel_tor * vel_pol
    term_mag = vel_tor * mag_pol - vel_pol * mag_tor
    grad_vtor = -vel_pol * adj_vel + mag_pol * adj_mag
    grad_vpol = -vel_tor * adj_vel - mag_tor * adj_mag
    grad_mtor = mag_pol * adj_vel - vel_pol * adj_mag
    grad_mpol = mag_tor * adj_vel + vel_tor * adj_mag
    cotangent_pair = jnp.stack([grad_vpol, grad_mpol])
    padded_back = jnp.pad(cotangent_pair, ((0, 0), (1, 1), (0, 0), (0, 0)))
    back_slopes = 0.5 * (padded_back[:, :-2] - padded_back[:, 2:])
    analysis_in = jnp.stack(
        [term_vel, term_mag, grad_vtor, back_slopes[0], grad_mtor, back_slopes[1]]
    ).astype(jnp.bfloat16)
    spectra_parts = []
    for start in range(0, WAVES, block_width):
        wave_block = wave_cosines(owner_list[start : start + block_width])
        spectra_parts.append(
            jnp.einsum(
                "crjf,smf->crsjm", analysis_in, wave_block, preferred_element_type=jnp.float32
            )
        )
    spectra = (norm_scale * jnp.concatenate(spectra_parts, axis=4)).astype(jnp.bfloat16)
    position = jnp.arange(NLAT, dtype=jnp.int32)
    returned = lax.all_to_all(
        lax.all_to_all(spectra, "ma", split_axis=4, concat_axis=3, tiled=True),
        "row",
        split_axis=1,
        concat_axis=3,
        tiled=True,
    )
    sub_rows = spectra.shape[3]
    radial_part = position // (owner_count * sub_rows)
    owner_part = position // sub_rows % owner_count
    theta_index = owner_part * (NLAT // owner_count) + radial_part * sub_rows + position % sub_rows
    back_table = lat_cosines(theta_index)
    result = jnp.einsum("crstk,tl->crskl", returned, back_table, preferred_element_type=jnp.float32)
    result = jnp.where(live_rows, result, 0.0)
    nonlinear = result[:2]
    seed_next = jnp.swapaxes(owned_seed, 3, 4).astype(jnp.float32) - step_size[0] * result[2:]
    return (nonlinear, seed_next)


def solution(mesh):
    return jax.shard_map(
        local,
        mesh=mesh,
        in_specs=(P(None, "row", None, "ma", None), P(None, "row", None, "ma", None), P(), P()),
        out_specs=(P(None, "row", None, "ma", None), P(None, "row", None, "ma", None)),
        check_vma=False,
    )
```

profile of v0, /device:TPU:0, one launch (start us, length us, event | category | flops | bytes accessed | tf_op | source)
XLA Modules:
  0.0 514.6 jit_solution(137748716376305591)
XLA Ops:
  2.0 4.3 copy.33
  6.3 6.0 %gather_fusion = bf16[1024,4,2,128]{3,1,2,0:T(4,128)(2,1)S(1)} fusion(bf16[4,2,128,1024]{2,0,3,1:T(4,128)(2,1)} %bitcast.294, s32[1024]{0:T(1024)S(1)} %fusion.223), kind=kCustom, calls=%fused_computation | custom fusion | bytes 4198400 | tf_op jit(solution)/shard_map/jit(_take)/gather | solution.py:37
  12.3 4.5 fusion.43
  16.8 6.5 %all-to-all-start = ((bf16[4,1,2,128,1024]{3,0,2,1,4:T(4,128)(2,1)}), bf16[4,1,2,128,1024]{3,0,2,1,4:T(4,128)(2,1)S(1)}, u32[]{:S(2)}, u32[]{:S(2)}) async-start(bf16[4,1,2,128,1024]{3,0,2,1,4:T(4,128)(2,1)} %fusion.43), calls=%async_computation | async-start | bytes 4194304 | tf_op jit(solution)/shard_map/all_to_all | solution.py:38
  23.6 17.5 %fusion.68 = bf16[2,1,2,1024,128]{4,3,2,0,1:T(8,128)(2,1)S(1)} fusion(s32[1024]{0:T(1024)S(1)} %multiply_add_fusion.1, bf16[2,1,2,128,1024]{4,3,2,1,0:T(8,128)(2,1)} %param.5, pred[128,1024]{1,0:T(8,128)(4,1)S(1)} %iota_compare_fusion.3), kind=kOutput, calls=%fused_computation.112 | convolution fusion | flops 1090519040 | bytes 2232320 | tf_op jit(solution)/shard_map/crskl,tl->crstk/dot_general | solution.py:46
  41.1 31.2 %all-to-all-done = bf16[4,1,2,128,1024]{3,0,2,1,4:T(4,128)(2,1)S(1)} async-done(((bf16[4,1,2,128,1024]{3,0,2,1,4:T(4,128)(2,1)}), bf16[4,1,2,128,1024]{3,0,2,1,4:T(4,128)(2,1)S(1)}, u32[]{:S(2)}, u32[]{:S(2)}) %all-to-all-start) | async-done | bytes 2097184 | tf_op jit(solution)/shard_map/all_to_all | solution.py:38
  72.3 3.0 copy.76
  75.3 19.5 %convert_bitcast_fusion = bf16[4,1,2,1024,128]{4,3,2,0,1:T(8,128)(2,1)S(1)} fusion(bf16[4,2,1024,128]{3,2,1,0:T(8,128)(2,1)} %bitcast.295, pred[1024,128]{1,0:T(8,128)(4,1)S(1)} %iota_compare_fusion.2, s32[1024]{0:T(1024)S(1)} %multiply_add_fusion.1), kind=kOutput, calls=%fused_computation.72 | convolution fusion | flops 2165309440 | bytes 4329472 | tf_op jit(solution)/shard_map/crslk,tl->crstk/dot_general | solution.py:40
  95.1 3.2 copy.37
  98.3 74.0 %all_to_all.87 = bf16[6,1,2,1024,128]{4,2,0,1,3:T(2,128)(2,1)S(1)} all-to-all(bf16[6,1,2,1024,128]{4,2,0,1,3:T(2,128)(2,1)S(1)} %copy.37), channel_id=1, replica_groups=mesh['ma'=8,'row'=4] {'ma'}, dimensions={3} | all-to-all | bytes 6291456 | tf_op jit(solution)/shard_map/all_to_all | solution.py:54
  172.3 2.2 copy.38
  174.4 4.7 copy.39
  179.1 8.6 %copy.40 = bf16[6,1,2,128,1024]{4,2,0,1,3:T(2,128)(2,1)} copy(bf16[6,1,2,128,1024]{3,4,2,0,1:T(8,128)(2,1)} %bitcast.284) | data formatting | bytes 6291456 | tf_op jit(solution)/shard_map/all_to_all | solution.py:54
  187.8 4.7 all-to-all-start.2
  192.4 5.7 %cosine_convert_fusion.6 = (bf16[1,128,2048]{2,1,0:T(8,128)(2,1)}, bf16[1,128,2048]{2,1,0:T(8,128)(2,1)}) fusion(s32[128]{0:T(128)S(1)} %get-tuple-element.17), kind=kLoop, calls=%fused_computation.216 | loop fusion | flops 4456448 | bytes 1049088 | tf_op jit(solution)/shard_map/convert.22
  198.1 5.6 %cosine_convert_fusion.7 = (bf16[1,128,2048]{2,1,0:T(8,128)(2,1)}, bf16[1,128,2048]{2,1,0:T(8,128)(2,1)}) fusion(s32[128]{0:T(128)S(1)} %get-tuple-element.20), kind=kLoop, calls=%fused_computation.222 | loop fusion | flops 4456448 | bytes 1049088 | tf_op jit(solution)/shard_map/convert.30
  203.8 9.8 %cosine_convert_fusion.2 = (bf16[1,128,2048]{2,1,0:T(8,128)(2,1)}, bf16[1,128,2048]{2,1,0:T(8,128)(2,1)}, bf16[1,128,2048]{2,1,0:T(8,128)(2,1)}, bf16[1,128,2048]{2,1,0:T(8,128)(2,1)}) fusion(s32[128]{0:T(128)S(1)} %get-tuple-element.19, s32[128]{0:T(128)S(1)} %get-tuple-element.18), kind=kLoop, calls=%fused_computation.200 | loop fusion | flops 8912896 | bytes 2098176 | tf_op jit(solution)/shard_map/convert.14
  213.6 9.8 %cosine_convert_fusion.4 = (bf16[1,128,2048]{2,1,0:T(8,128)(2,1)}, bf16[1,128,2048]{2,1,0:T(8,128)(2,1)}, bf16[1,128,2048]{2,1,0:T(8,128)(2,1)}, bf16[1,128,2048]{2,1,0:T(8,128)(2,1)}) fusion(s32[128]{0:T(128)S(1)} %get-tuple-element.15, s32[128]{0:T(128)S(1)} %get-tuple-element.16), kind=kLoop, calls=%fused_computation.208 | loop fusion | flops 8912896 | bytes 2098176 | tf_op jit(solution)/shard_map/convert.18
  223.4 9.8 %cosine_convert_fusion = (bf16[1,128,2048]{2,1,0:T(8,128)(2,1)S(1)}, bf16[1,128,2048]{2,1,0:T(8,128)(2,1)S(1)}, bf16[1,128,2048]{2,1,0:T(8,128)(2,1)}, bf16[1,128,2048]{2,1,0:T(8,128)(2,1)}) fusion(s32[128]{0:T(128)S(1)} %get-tuple-element.14, s32[128]{0:T(128)S(1)} %get-tuple-element.22), kind=kLoop, calls=%fused_computation.192 | loop fusion | flops 8912896 | bytes 2098176 | tf_op jit(solution)/shard_map/convert.10
  233.3 2.9 copy.84
  236.3 3.7 fusion.153
  239.9 3.7 fusion.155
  243.6 3.6 fusion.157
  247.2 3.7 fusion.159
  250.9 3.6 fusion.151
  254.5 3.7 fusion.161
  258.2 3.7 fusion.163
  261.9 18.1 %fusion = f32[6,4,32,2048]{3,2,1,0:T(8,128)} fusion(f32[6,4,32,2048,1]{3,2,4,1,0:T(8,128)} %fusion.151, f32[6,4,32,2048,1]{3,2,4,1,0:T(8,128)} %fusion.153, f32[6,4,32,2048,1]{3,2,4,1,0:T(8,128)} %fusion.155, f32[6,4,32,2048,1]{3,2,4,1,0:T(8,128)} %fusion.157, f32[6,4,32,2048,1]{3,2,4,1,0:T(8,128)} %fusion.159, f32[6,4,32,2048,1]{3,2,4,1,0:T(8,128)} %fusion.161, ...), kind=kOutput, calls=%fused_computation.2 | convolution fusion | flops 818413568 | bytes 51773440 | tf_op jit(solution)/shard_map/crsjm,smf->crjf/dot_general | solution.py:63
  280.1 3.4 multiply_subtract_fusion
  284.8 1.2 slice-done
  296.1 1.0 fusion.110
  297.1 1.0 fusion.116
  298.1 2.6 multiply_convert_fusion
  300.7 19.5 %copy.43 = bf16[6,4,2,32,1024]{3,1,0,2,4:T(4,128)(2,1)} copy(bf16[6,4,2,32,1024]{4,3,1,0,2:T(8,128)(2,1)} %multiply_convert_fusion) | data formatting | bytes 6291456 | tf_op jit(solution)/shard_map/convert_element_type | solution.py:100
  320.2 14.5 %reshape.933 = bf16[8,2,98304]{2,1,0:T(2,128)(2,1)} reshape(bf16[1024,2,6,4,32]{4,3,2,1,0:T(4,128)(2,1)} %bitcast.279) | data formatting | bytes 6291456
  334.7 75.9 %all_to_all.88 = bf16[8,2,98304]{2,1,0:T(2,128)(2,1)} all-to-all(bf16[8,2,98304]{2,1,0:T(2,128)(2,1)} %reshape.933), channel_id=1, replica_groups=mesh['ma'=8,'row'=4] {'ma'}, dimensions={0} | all-to-all | bytes 6291456 | tf_op jit(solution)/shard_map/all_to_all | solution.py:103
  410.7 10.7 %reshape.934 = bf16[1024,2,6,4,32]{4,3,2,1,0:T(4,128)(2,1)} reshape(bf16[8,2,98304]{2,1,0:T(2,128)(2,1)} %all_to_all.88) | data formatting | bytes 6291456
  421.4 17.7 %copy.81 = bf16[6,4,2,32,8,128]{5,3,4,2,0,1:T(8,128)(2,1)} copy(bf16[6,4,2,32,8,128]{3,1,0,2,5,4:T(4,128)(2,1)} %bitcast.280) | data formatting | bytes 6291456 | tf_op jit(solution)/shard_map/all_to_all | solution.py:103
  439.1 4.7 all-to-all-start.4
  444.4 3.2 bitcast_convert_fusion
  447.6 4.9 reshape.902
  452.5 27.5 %all-to-all-done.4 = bf16[6,4,2,256,128]{4,3,2,0,1:T(8,128)(2,1)} async-done(((bf16[6,4,2,256,128]{4,3,2,0,1:T(8,128)(2,1)}), bf16[6,4,2,256,128]{4,3,2,0,1:T(8,128)(2,1)}, u32[]{:S(2)}, u32[]{:S(2)}) %all-to-all-start.4) | async-done | bytes 3145760 | tf_op jit(solution)/shard_map/all_to_all | solution.py:102
  480.0 4.4 copy.47
  484.5 4.0 reshape.901
  488.5 19.9 %broadcast_select_fusion = f32[6,2,128,1024]{3,2,1,0:T(8,128)S(1)} fusion(pred[128,1024]{1,0:T(8,128)(4,1)S(1)} %iota_compare_fusion.3, bf16[6,2,1024,128]{2,3,1,0:T(8,128)(2,1)} %reshape.901, s32[1024]{0:T(1024)S(1)} %fusion.218), kind=kOutput, calls=%fused_computation.58 | convolution fusion | flops 3238526976 | bytes 9572352 | tf_op jit(solution)/shard_map/crstk,tl->crskl/dot_general | solution.py:114
  508.4 1.5 slice_bitcast_fusion
  509.9 1.5 copy-done
  511.4 3.0 fusion.13
  (90 shorter events, 13.3 us)
Async XLA Ops:
  16.8 6.5 %copy-start.30 = (s32[1024]{0:T(1024)S(1)}, s32[1024]{0:T(1024)}, u32[]{:S(2)}) copy-start(s32[1024]{0:T(1024)} %param.7) | copy-start | bytes 12292
  16.8 55.5 %all-to-all-start = ((bf16[4,1,2,128,1024]{3,0,2,1,4:T(4,128)(2,1)}), bf16[4,1,2,128,1024]{3,0,2,1,4:T(4,128)(2,1)S(1)}, u32[]{:S(2)}, u32[]{:S(2)}) async-start(bf16[4,1,2,128,1024]{3,0,2,1,4:T(4,128)(2,1)} %fusion.43), calls=%async_computation | async-start | bytes 4194304 | tf_op jit(solution)/shard_map/all_to_all | solution.py:38
  187.8 45.5 %all-to-all-start.2 = ((bf16[6,1,2,128,1024]{4,2,0,1,3:T(2,128)(2,1)}), bf16[6,1,2,128,1024]{4,2,0,1,3:T(2,128)(2,1)}, u32[]{:S(2)}, u32[]{:S(2)}) async-start(bf16[6,1,2,128,1024]{4,2,0,1,3:T(2,128)(2,1)} %copy.40), calls=%async_computation.2 | async-start | bytes 6291456 | tf_op jit(solution)/shard_map/all_to_all | solution.py:53
  233.2 3.0 copy-start.10
  233.2 3.0 copy-start.12
  236.2 22.0 %copy-start.1 = (bf16[6,1,2,4,32,1024]{5,4,2,3,0,1:T(8,128)(2,1)}, bf16[6,1,2,4,32,1024]{5,4,2,3,0,1:T(8,128)(2,1)S(1)}, u32[]{:S(2)}) copy-start(bf16[6,1,2,4,32,1024]{5,4,2,3,0,1:T(8,128)(2,1)S(1)} %copy.84) | copy-start | bytes 9437188
  236.2 3.7 copy-start.14
  236.2 3.7 copy-start.16
  239.9 3.7 copy-start.22
  239.9 3.7 copy-start.24
  243.6 3.6 copy-start.26
  243.6 3.6 copy-start.28
  247.2 3.7 copy-start.18
  247.2 3.7 copy-start.20
  250.9 3.6 copy-start.2
  250.9 3.6 copy-start.4
  254.5 3.7 copy-start.6
  254.5 3.7 copy-start.8
  283.8 2.2 slice-start
  284.1 2.6 slice-start.1
  287.7 1.0 copy-start.7
  287.7 1.2 copy-start.9
  288.9 1.0 copy-start.3
  288.9 1.2 copy-start.5
  290.1 1.0 copy-start.27
  290.1 1.2 copy-start.29
  291.3 1.0 copy-start.23
  291.3 1.2 copy-start.25
  292.5 1.0 copy-start.15
  292.5 1.2 copy-start.17
  293.7 1.0 copy-start.11
  293.7 1.2 copy-start.13
  294.9 1.0 copy-start.19
  294.9 1.2 copy-start.21
  439.1 41.0 %all-to-all-start.4 = ((bf16[6,4,2,256,128]{4,3,2,0,1:T(8,128)(2,1)}), bf16[6,4,2,256,128]{4,3,2,0,1:T(8,128)(2,1)}, u32[]{:S(2)}, u32[]{:S(2)}) async-start(bf16[6,4,2,256,128]{4,3,2,0,1:T(8,128)(2,1)} %bitcast.293), calls=%async_computation.4 | async-start | bytes 6291456 | tf_op jit(solution)/shard_map/all_to_all | solution.py:102
  508.4 2.9 copy-start
where the time goes:
time: 525 us; the launch traced here: 515 us
  blocking collectives  150 us (29%)
  local copies, waits for them, and re-layouts  118 us (22%)
  matrix products  109 us (21%)
  other arithmetic  61.8 us (12%)
  waiting for transfers between devices  58.7 us (11%)
  starting transfers between devices  15.8 us (3%)
    all_to_all x1, blocking collectives, local(): lax.all_to_all(spectra, 'ma', split_axis=4, concat_axis=3, tiled=True)  75.9 us
    all_to_all x1, blocking collectives, local(): lax.all_to_all(spec_rows, 'ma', split_axis=3, concat_axis=4, tiled=True)  74 us
    dot_general x8, matrix products, local(): jnp.einsum('crsjm,smf->crjf', gridded[..., start:start + block_width], wa...  43.8 us
    another operation x6, other arithmetic  41 us
    unnamed x71, local copies, waits for them, and re-layouts  36.4 us
    all_to_all x1, waiting for transfers between devices, local(): lax.all_to_all(listed, 'ma', split_axis=4, concat_axis=3, tiled=True)  31.2 us
    all_to_all x1, waiting for transfers between devices, local(): lax.all_to_all(lax.all_to_all(spectra, 'ma', split_axis=4, concat_axis=3,...  27.5 us
    dot_general x1, matrix products, local(): jnp.einsum('crstk,tl->crskl', returned, back_table, preferred_element_typ...  19.9 us
  transfers between devices with their start and end apart: 3, of which 2 were waited for; matrix products, arithmetic and copies ran while one was open for 13% of the time, Pallas kernels for 0%

commit v1 on v0

--- a/solution.py
+++ b/solution.py
@@ -1,14 +1,20 @@
+import functools
 import math
 
 import jax
 import jax.numpy as jnp
 from jax import lax
+from jax.experimental import pallas as pl
+from jax.experimental.pallas import tpu as pltpu
 from jax.sharding import PartitionSpec as P
 
 WAVES = 1024
 DEGREES = 1024
 NLAT = 1024
 NLON = 2048
+F_TILE = 256
+BF16 = jnp.bfloat16
+F32 = jnp.float32
 
 
 def lat_cosines(theta_index):
@@ -24,7 +30,320 @@
     return jnp.stack([jnp.cos(angles), -jnp.sin(angles)]).astype(jnp.bfloat16)
 
 
+def cos_sin(phase_index, period):
+    angles = (phase_index % period).astype(F32) * (2.0 * math.pi / period)
+    return jnp.cos(angles), jnp.sin(angles)
+
+
+def lat_table_of():
+    step = 32
+    degree = jnp.arange(DEGREES, dtype=jnp.int32)
+    coarse = jnp.arange(NLAT // step, dtype=jnp.int32)
+    fine = jnp.arange(step, dtype=jnp.int32)
+    cos_a, sin_a = cos_sin(2 * step * coarse[:, None] * degree[None, :], 4 * NLAT)
+    cos_b, sin_b = cos_sin((2 * fine[:, None] + 1) * degree[None, :], 4 * NLAT)
+    table = cos_a[:, None, :] * cos_b[None, :, :] - sin_a[:, None, :] * sin_b[None, :, :]
+    return table.astype(BF16).reshape(NLAT, DEGREES)
+
+
+def wave_table_of(owner_list):
+    tiles = jnp.arange(NLON // F_TILE, dtype=jnp.int32)
+    fine = jnp.arange(F_TILE, dtype=jnp.int32)
+    cos_a, sin_a = cos_sin(F_TILE * tiles[:, None] * owner_list[None, :], NLON)
+    cos_b, sin_b = cos_sin(owner_list[:, None] * fine[None, :], NLON)
+    cos_a, sin_a = cos_a[:, :, None], sin_a[:, :, None]
+    cosine = cos_a * cos_b[None] - sin_a * sin_b[None]
+    minus_sine = -sin_a * cos_b[None] - cos_a * sin_b[None]
+    table = jnp.stack([cosine.astype(BF16), minus_sine.astype(BF16)], axis=1)
+    return table.reshape(NLON // F_TILE, 2 * WAVES, F_TILE)
+
+
+def estimate(flops, bytes_accessed):
+    return pl.CostEstimate(flops=flops, bytes_accessed=bytes_accessed, transcendentals=0)
+
+
+def permute_kernel(owner_ref, seed_ref, out_ref):
+    chans, _, parts, lines, waves = seed_ref.shape
+    group, own = out_ref.shape[0], out_ref.shape[4]
+    rows = seed_ref[...].reshape(chans * parts * lines, waves)
+    wave = lax.broadcasted_iota(jnp.int32, (waves, group * own), 0)
+    one_hot = jnp.where(wave == owner_ref[...], 1.0, 0.0).astype(BF16)
+    picked = jnp.dot(rows, one_hot, preferred_element_type=F32).astype(BF16)
+    for d in range(group):
+        part = picked[:, d * own : (d + 1) * own]
+        out_ref[d] = part.reshape(chans, parts, lines, own)
+
+
+def permute(seed_field, owner_list, owners):
+    chans, radii, parts, lines, waves = seed_field.shape
+    own = waves // owners
+    group = 2 if owners % 2 == 0 else 1
+    return pl.pallas_call(
+        permute_kernel,
+        grid=(owners // group,),
+        in_specs=[
+            pl.BlockSpec((1, group * own), lambda i: (0, i)),
+            pl.BlockSpec((chans, radii, parts, lines, waves), lambda i: (0, 0, 0, 0, 0)),
+        ],
+        out_specs=pl.BlockSpec((group, chans, parts, lines, own), lambda i: (i, 0, 0, 0, 0)),
+        out_shape=jax.ShapeDtypeStruct((owners, chans, parts, lines, own), BF16),
+        cost_estimate=estimate(2 * chans * parts * lines * waves * waves, 4 * seed_field.size),
+        name="permute",
+    )(owner_list.reshape(1, waves), seed_field)
+
+
+def adjoint_rows_kernel(waves_ref, lat_ref, cot_ref, out_ref):
+    parts, own, degrees = cot_ref.shape[2:]
+    devices, _, _, sub, _ = out_ref.shape
+    live = lax.broadcasted_iota(jnp.int32, (own, degrees), 1) >= waves_ref[...]
+    for s in range(parts):
+        coeffs = jnp.where(live, cot_ref[0, 0, s], jnp.zeros((), BF16))
+        rows = lax.dot_general(
+            lat_ref[...], coeffs, (((1,), (1,)), ((), ())), preferred_element_type=F32
+        )
+        out_ref[:, 0, s] = rows.astype(BF16).reshape(devices, sub, own)
+
+
+def forward_rows_kernel(waves_ref, lat_ref, seed_ref, base_ref, out_ref):
+    del base_ref
+    owners, _, parts, lines, own = seed_ref.shape
+    devices, _, _, sub, _ = out_ref.shape
+    degrees = owners * lines
+    live = lax.broadcasted_iota(jnp.int32, (degrees, own), 0) >= waves_ref[...]
+    coeffs = jnp.concatenate(
+        [
+            jnp.where(live, seed_ref[:, 0, s].reshape(degrees, own), jnp.zeros((), BF16))
+            for s in range(parts)
+        ],
+        axis=1,
+    )
+    rows = jnp.dot(lat_ref[...], coeffs, preferred_element_type=F32).astype(BF16)
+    for s in range(parts):
+        out_ref[:, 0, s] = rows[:, s * own : (s + 1) * own].reshape(devices, sub, own)
+
+
+def adjoint_rows(my_waves, lat_table, cotangent, seed_chans, devices):
+    chans, _, parts, own, degrees = cotangent.shape
+    sub = NLAT // devices
+    return pl.pallas_call(
+        adjoint_rows_kernel,
+        grid=(chans,),
+        in_specs=[
+            pl.BlockSpec((own, 1), lambda c: (0, 0)),
+            pl.BlockSpec((NLAT, degrees), lambda c: (0, 0)),
+            pl.BlockSpec((1, 1, parts, own, degrees), lambda c: (c, 0, 0, 0, 0)),
+        ],
+        out_specs=pl.BlockSpec(
+            (devices, 1, parts, sub, own), lambda c: (0, seed_chans + c, 0, 0, 0)
+        ),
+        out_shape=jax.ShapeDtypeStruct((devices, seed_chans + chans, parts, sub, own), BF16),
+        cost_estimate=estimate(2 * cotangent.size * NLAT, 4 * cotangent.size + 2 * lat_table.size),
+        name="adjoint_rows",
+    )(my_waves.reshape(own, 1), lat_table, cotangent)
+
+
+def forward_rows(my_waves, lat_table, owned_seed, base):
+    owners, chans, parts, lines, own = owned_seed.shape
+    devices, _, _, sub, _ = base.shape
+    return pl.pallas_call(
+        forward_rows_kernel,
+        grid=(chans,),
+        in_specs=[
+            pl.BlockSpec((1, own), lambda c: (0, 0)),
+            pl.BlockSpec((NLAT, owners * lines), lambda c: (0, 0)),
+            pl.BlockSpec((owners, 1, parts, lines, own), lambda c: (0, c, 0, 0, 0)),
+            pl.BlockSpec(memory_space=pl.ANY),
+        ],
+        out_specs=pl.BlockSpec((devices, 1, parts, sub, own), lambda c: (0, c, 0, 0, 0)),
+        out_shape=jax.ShapeDtypeStruct(base.shape, BF16),
+        input_output_aliases={3: 0},
+        cost_estimate=estimate(2 * owned_seed.size * NLAT, 4 * owned_seed.size + 2 * lat_table.size),
+        name="forward_rows",
+    )(my_waves.reshape(1, own), lat_table, owned_seed, base)
+
+
+def slope(values):
+    rim = jnp.zeros_like(values[:1])
+    upper = jnp.concatenate([values[1:], rim], axis=0)
+    lower = jnp.concatenate([rim, values[:-1]], axis=0)
+    return 0.5 * (upper - lower)
+
+
+def grid_kernel(f_tiles, norm_scale, got_ref, tab_ref, back_tab_ref, out_ref, rows_ref, terms_ref):
+    step = pl.program_id(0)
+    devices, chans, parts, sub, own = got_ref.shape
+    radii = rows_ref.shape[1]
+    owners = devices // radii
+    rows = chans * radii * sub
+    group = out_ref.shape[0] // radii
+
+    @pl.when(step == 0)
+    def _():
+        for s in range(parts):
+            for d in range(owners):
+                start = (s * owners + d) * own
+                for r in range(radii):
+                    rows_ref[:, r, :, start : start + own] = got_ref[d * radii + r, :, s]
+
+    @pl.when(step < f_tiles)
+    def _():
+        field = norm_scale * jnp.dot(
+            rows_ref[...].reshape(rows, -1), tab_ref[0], preferred_element_type=F32
+        )
+        field = field.reshape(chans, radii, sub, F_TILE)
+        vel_tor = field[0]
+        vel_pol = slope(field[1])
+        mag_tor = field[2]
+        mag_pol = slope(field[3])
+        adj_vel = field[4]
+        adj_mag = field[5]
+        grad_vpol = -vel_tor * adj_vel - mag_tor * adj_mag
+        grad_mpol = mag_tor * adj_vel + vel_tor * adj_mag
+        terms = [
+            mag_tor * mag_pol - vel_tor * vel_pol,
+            vel_tor * mag_pol - vel_pol * mag_tor,
+            -vel_pol * adj_vel + mag_pol * adj_mag,
+            -slope(grad_vpol),
+            mag_pol * adj_vel - vel_pol * adj_mag,
+            -slope(grad_mpol),
+        ]
+        for c, term in enumerate(terms):
+            terms_ref[step, c] = term.astype(BF16)
+
+    @pl.when(step >= f_tiles)
+    def _():
+        total = None
+        for a in range(f_tiles):
+            part = lax.dot_general(
+                terms_ref[a].reshape(rows, F_TILE),
+                back_tab_ref[a],
+                (((1,), (1,)), ((), ())),
+                preferred_element_type=F32,
+            )
+            total = part if total is None else total + part
+        back = (norm_scale * total).astype(BF16).reshape(chans, radii, sub, group * own)
+        for d in range(group):
+            for r in range(radii):
+                out_ref[d * radii + r, :, 0] = back[:, r, :, d * own : (d + 1) * own]
+
+
+def grid_step(got, table, radii):
+    devices, chans, parts, sub, own = got.shape
+    owners = devices // radii
+    f_tiles, waves_wide, _ = table.shape
+    group = 2 if owners % 2 == 0 else 1
+    per_part = owners // group
+    norm_scale = 2.0 / math.sqrt(DEGREES * WAVES)
+
+    def back(i):
+        return jnp.maximum(i - f_tiles, 0)
+
+    return pl.pallas_call(
+        functools.partial(grid_kernel, f_tiles, norm_scale),
+        grid=(f_tiles + parts * per_part,),
+        in_specs=[
+            pl.BlockSpec(got.shape, lambda i: (0, 0, 0, 0, 0)),
+            pl.BlockSpec((1, waves_wide, F_TILE), lambda i: (jnp.minimum(i, f_tiles - 1), 0, 0)),
+            pl.BlockSpec((f_tiles, group * own, F_TILE), lambda i: (0, back(i), 0)),
+        ],
+        out_specs=pl.BlockSpec(
+            (group * radii, chans, 1, sub, own),
+            lambda i: (back(i) % per_part, 0, back(i) // per_part, 0, 0),
+        ),
+        out_shape=jax.ShapeDtypeStruct(got.shape, BF16),
+        scratch_shapes=[
+            pltpu.VMEM((chans, radii, sub, waves_wide), BF16),
+            pltpu.VMEM((f_tiles, chans, radii, sub, F_TILE), BF16),
+        ],
+        cost_estimate=estimate(
+            4 * chans * radii * sub * waves_wide * NLON, 4 * got.size + 4 * table.size
+        ),
+        name="grid_step",
+    )(got, table, table)
+
+
+def result_kernel(pair, step_ref, waves_ref, lat_ref, back_ref, listed_ref, non_ref, next_ref):
+    block = pl.program_id(0)
+    devices, _, parts, sub, own = back_ref.shape
+    degrees = lat_ref.shape[1]
+    live = lax.broadcasted_iota(jnp.int32, (own, degrees), 1) >= waves_ref[...]
+    columns = jnp.concatenate(
+        [
+            back_ref[:, c, s].reshape(devices * sub, own)
+            for c in range(pair)
+            for s in range(parts)
+        ],
+        axis=1,
+    )
+    result = lax.dot_general(
+        columns, lat_ref[...], (((0,), (0,)), ((), ())), preferred_element_type=F32
+    )
+    for c in range(pair):
+        for s in range(parts):
+            start = (c * parts + s) * own
+            value = jnp.where(live, result[start : start + own], 0.0)
+
+            @pl.when(block == 0)
+            def _(value=value, c=c, s=s):
+                non_ref[c, 0, s] = value
+
+            @pl.when(block > 0)
+            def _(value=value, c=c, s=s):
+                next_ref[c, 0, s] = listed_ref[c, s].astype(F32) - step_ref[0] * value
+
+
+def results(step_size, my_waves, lat_table, returned, listed):
+    devices, chans, parts, sub, own = returned.shape
+    degrees = lat_table.shape[1]
+    pair = 2
+    seed_chans = listed.shape[0]
+
+    def seed_block(i):
+        return jnp.maximum(i - 1, 0)
+
+    return pl.pallas_call(
+        functools.partial(result_kernel, pair),
+        grid=(chans // pair,),
+        in_specs=[
+            pl.BlockSpec(memory_space=pltpu.SMEM),
+            pl.BlockSpec((own, 1), lambda i: (0, 0)),
+            pl.BlockSpec(lat_table.shape, lambda i: (0, 0)),
+            pl.BlockSpec((devices, pair, parts, sub, own), lambda i: (0, i, 0, 0, 0)),
+            pl.BlockSpec((pair, parts, own, degrees), lambda i: (seed_block(i), 0, 0, 0)),
+        ],
+        out_specs=[
+            pl.BlockSpec((pair, 1, parts, own, degrees), lambda i: (0, 0, 0, 0, 0)),
+            pl.BlockSpec((pair, 1, parts, own, degrees), lambda i: (seed_block(i), 0, 0, 0, 0)),
+        ],
+        out_shape=[
+            jax.ShapeDtypeStruct((chans - seed_chans, 1, parts, own, degrees), F32),
+            jax.ShapeDtypeStruct((seed_chans, 1, parts, own, degrees), F32),
+        ],
+        cost_estimate=estimate(2 * returned.size * degrees, 2 * returned.size + 4 * returned.size),
+        name="results",
+    )(step_size, my_waves.reshape(own, 1), lat_table, returned, listed)
+
+
 def local(seed_field, cotangent, step_size, owner_list):
+    owners, radii = lax.axis_size("ma"), lax.axis_size("row")
+    own = cotangent.shape[3]
+    my_waves = lax.dynamic_slice_in_dim(owner_list, lax.axis_index("ma") * own, own)
+    permuted = permute(seed_field, owner_list, owners)
+    owned_seed = lax.all_to_all(permuted, "ma", 0, 0, tiled=True)
+    lat_table = lat_table_of()
+    wave_table = wave_table_of(owner_list)
+    base = adjoint_rows(my_waves, lat_table, cotangent, seed_field.shape[0], owners * radii)
+    spec_rows = forward_rows(my_waves, lat_table, owned_seed, base)
+    gridded = lax.all_to_all(spec_rows, ("ma", "row"), 0, 0, tiled=True)
+    listed = jnp.transpose(owned_seed, (1, 2, 4, 0, 3))
+    listed = listed.reshape(listed.shape[:3] + (DEGREES,))
+    back_rows = grid_step(gridded, wave_table, radii)
+    returned = lax.all_to_all(back_rows, ("ma", "row"), 0, 0, tiled=True)
+    nonlinear, seed_next = results(step_size, my_waves, lat_table, returned, listed)
+    return (nonlinear, seed_next)
+
+
+def local_small(seed_field, cotangent, step_size, owner_list):
     owner_count = lax.axis_size("ma")
     own_waves = cotangent.shape[3]
     norm_scale = 2.0 / math.sqrt(DEGREES * WAVES)
@@ -118,9 +437,15 @@
     return (nonlinear, seed_next)
 
 
+def fits(mesh):
+    owners, radii = mesh.shape["ma"], mesh.shape["row"]
+    own, sub = WAVES // owners, NLAT // (owners * radii)
+    return own % 128 == 0 and sub % 16 == 0
+
+
 def solution(mesh):
     return jax.shard_map(
-        local,
+        local if fits(mesh) else local_small,
         mesh=mesh,
         in_specs=(P(None, "row", None, "ma", None), P(None, "row", None, "ma", None), P(), P()),
         out_specs=(P(None, "row", None, "ma", None), P(None, "row", None, "ma", None)),

time: 525 us -> 253 us (0.48); the launches traced: 515 us -> 253 us
  blocking collectives: 150 us -> 0 us
  matrix products: 109 us -> 0 us
  local copies, waits for them, and re-layouts: 118 us -> 9.36 us
  waiting for transfers between devices: 58.7 us -> 158 us
  Pallas kernels: 0 us -> 49.1 us
  other arithmetic: 61.8 us -> 19.4 us
    all_to_all x2 -> x0, blocking collectives: 150 us -> none  [the longest x1 75.9 us: local(): lax.all_to_all(spectra, 'ma', split_axis=4, concat_axis=3, tiled=True)]
    dot_general x19 -> x0, matrix products: 109 us -> none  [the longest x8 43.8 us: local(): jnp.einsum('crsjm,smf->crjf', gridded[..., start:start + block_width], wa...]
    all_to_all x3, waiting for transfers between devices: 58.7 us -> 158 us  [the longest x1 63.8 us: local(): returned = lax.all_to_all(back_rows, ('ma', 'row'), 0, 0, tiled=True)]
    pallas_call x0 -> x5, Pallas kernels: none -> 49.1 us  [the longest x1 23.2 us: grid_step(): pl.pallas_call(functools.partial(grid_kernel, f_tiles, norm_scale), grid=...]
    all_to_all x7 -> x0, local copies, waits for them, and re-layouts: 43.6 us -> none  [the longest x1 17.7 us: local(): lax.all_to_all(spectra, 'ma', split_axis=4, concat_axis=3, tiled=True)]
    another operation x8 -> x1, other arithmetic: 41.7 us -> 6.18 us  [wave_table_of(): table = jnp.stack([cosine.astype(BF16), minus_sine.astype(BF16)], axis=1)]
    unnamed x71 -> x6, local copies, waits for them, and re-layouts: 36.4 us -> 1.33 us
    convert_element_type x2 -> x0, local copies, waits for them, and re-layouts: 24.4 us -> none  [the longest x1 19.5 us: local(): (norm_scale * jnp.concatenate(spectra_parts, axis=4)).astype(jnp.bfloat16)]
  transfers between devices with their start and end apart: 3 -> 3, of which waited for: 2 -> 3; matrix products, arithmetic and copies ran while one was open for 13% -> 11% of each run, Pallas kernels for 0% -> 2%
where the time goes in v1:
time: 253 us
  waiting for transfers between devices  158 us (62%)
  Pallas kernels  49.1 us (19%)
  other arithmetic  19.4 us (8%)
  starting transfers between devices  15.5 us (6%)
  local copies, waits for them, and re-layouts  9.36 us (4%)
    all_to_all x1, waiting for transfers between devices, local(): returned = lax.all_to_all(back_rows, ('ma', 'row'), 0, 0, tiled=True)  63.8 us
    all_to_all x1, waiting for transfers between devices, local(): gridded = lax.all_to_all(spec_rows, ('ma', 'row'), 0, 0, tiled=True)  54.8 us
    all_to_all x1, waiting for transfers between devices, local(): owned_seed = lax.all_to_all(permuted, 'ma', 0, 0, tiled=True)  39.2 us
    pallas_call x1, Pallas kernels, grid_step(): pl.pallas_call(functools.partial(grid_kernel, f_tiles, norm_scale), grid=...  23.2 us
    pallas_call x1, Pallas kernels, results(): pl.pallas_call(functools.partial(result_kernel, pair), grid=(chans // pai...  9.21 us
    all_to_all x1, starting transfers between devices, local(): owned_seed = lax.all_to_all(permuted, 'ma', 0, 0, tiled=True)  6.35 us
    another operation x1, other arithmetic, wave_table_of(): table = jnp.stack([cosine.astype(BF16), minus_sine.astype(BF16)], axis=1)  6.18 us
    pallas_call x1, Pallas kernels, forward_rows(): pl.pallas_call(forward_rows_kernel, grid=(chans,), in_specs=[pl.BlockSpec...  6.09 us
  transfers between devices with their start and end apart: 3, of which 3 were waited for; matrix products, arithmetic and copies ran while one was open for 11% of the time, Pallas kernels for 2%

profile of v1, /device:TPU:0, one launch (start us, length us, event | category | flops | bytes accessed | tf_op | source)
XLA Modules:
  0.0 252.5 jit_solution(17658350075914393067)
XLA Ops:
  0.6 0.0 copy-start.2
  0.6 5.4 %permute.1 = bf16[8,4,2,128,128]{4,3,2,1,0:T(8,128)(2,1)} custom-call(s32[1,1024]{1,0:T(1,128)} %bitcast.16, bf16[4,1,2,128,1024]{4,3,2,1,0:T(8,128)(2,1)} %seed_ref.1), custom_call_target="tpu_custom_call" | custom-call | flops 2147483648 | bytes 4194304 | tf_op jit(solution)/shard_map/permute/pallas_call | solution.py:81
  6.0 6.4 %all-to-all-start = ((bf16[8,4,2,128,128]{4,3,2,1,0:T(8,128)(2,1)}), bf16[8,4,2,128,128]{4,3,2,1,0:T(8,128)(2,1)S(1)}, u32[]{:S(2)}, u32[]{:S(2)}) async-start(bf16[8,4,2,128,128]{4,3,2,1,0:T(8,128)(2,1)} %permute.1), calls=%async_computation | async-start | bytes 4194304 | tf_op jit(solution)/shard_map/all_to_all | solution.py:332
  12.4 0.0 copy-done.2
  12.4 0.6 dynamic-slice_bitcast_fusion
  13.0 0.7 copy.9.waves_ref
  13.7 1.1 fusion.21
  14.8 2.1 subtract_convert_fusion.2
  16.9 5.3 %adjoint_rows.1.base_ref = bf16[32,6,2,32,128]{4,3,2,1,0:T(8,128)(2,1)} custom-call(s32[128,1]{1,0:T(8,128)} %copy.9.waves_ref, bf16[1024,1024]{1,0:T(8,128)(2,1)} %bitcast.10, bf16[2,1,2,128,1024]{4,3,2,1,0:T(8,128)(2,1)} %cot_ref.1), custom_call_target="tpu_custom_call" | custom-call | flops 1073741824 | bytes 4194304 | tf_op jit(solution)/shard_map/adjoint_rows/pallas_call | solution.py:128
  22.2 39.2 %all-to-all-done.seed_ref = bf16[8,4,2,128,128]{4,3,2,1,0:T(8,128)(2,1)S(1)} async-done(((bf16[8,4,2,128,128]{4,3,2,1,0:T(8,128)(2,1)}), bf16[8,4,2,128,128]{4,3,2,1,0:T(8,128)(2,1)S(1)}, u32[]{:S(2)}, u32[]{:S(2)}) %all-to-all-start) | async-done | bytes 2097184 | tf_op jit(solution)/shard_map/all_to_all | solution.py:332
  61.4 0.0 copy-start
  61.4 1.3 copy-done
  62.7 6.1 %forward_rows.1 = bf16[32,6,2,32,128]{4,3,2,1,0:T(8,128)(2,1)} custom-call(s32[1,128]{1,0:T(1,128)} %get-tuple-element.9.waves_ref, bf16[1024,1024]{1,0:T(8,128)(2,1)} %bitcast.11, bf16[8,4,2,128,128]{4,3,2,1,0:T(8,128)(2,1)} %copy-done, bf16[32,6,2,32,128]{4,3,2,1,0:T(8,128)(2,1)} %adjoint_rows.1.base_ref), custom_call_target="tpu_custom_call", output_to_operand_aliasing={{}: (3, {})} | custom-call | flops 2147483648 | bytes 6291456 | tf_op jit(solution)/shard_map/forward_rows/pallas_call | solution.py:148
  68.8 3.8 %all-to-all-start.1 = ((bf16[32,6,2,32,128]{4,3,2,1,0:T(8,128)(2,1)}), bf16[32,6,2,32,128]{4,3,2,1,0:T(8,128)(2,1)}, u32[]{:S(2)}, u32[]{:S(2)}) async-start(bf16[32,6,2,32,128]{4,3,2,1,0:T(8,128)(2,1)} %forward_rows.1), calls=%async_computation.1 | async-start | bytes 6291456 | tf_op jit(solution)/shard_map/all_to_all | solution.py:337
  72.7 0.2 fusion.27
  72.9 4.2 %fusion.7 = (f32[1024,256]{1,0:T(8,128)S(1)}, f32[1024,256]{1,0:T(8,128)S(1)}) fusion(s32[1024]{0:T(1024)S(1)} %copy-done.2), kind=kLoop, calls=%fused_computation.14 | loop fusion | flops 3670016 | bytes 2101248 | tf_op jit(solution)/shard_map/cos | solution.py:35
  77.1 5.6 %subtract_convert_fusion.1 = (bf16[8,1,1024,256]{3,2,1,0:T(8,128)(2,1)S(1)}, bf16[8,1,1024,256]{3,2,1,0:T(8,128)(2,1)}) fusion(f32[1024,256]{1,0:T(8,128)S(1)} %get-tuple-element.8, f32[8,1024]{1,0:T(8,128)S(1)} %get-tuple-element.4, f32[1024,256]{1,0:T(8,128)S(1)} %get-tuple-element.7, f32[8,1024]{1,0:T(8,128)S(1)} %get-tuple-element.6, ...), kind=kLoop, calls=%fused_computation.2 | loop fusion | flops 16777216 | bytes 10584064 | tf_op jit(solution)/shard_map/convert_element_type | solution.py:57
  82.6 6.2 %pad_maximum_fusion = bf16[8,2,1024,256]{3,2,1,0:T(8,128)(2,1)} fusion(bf16[8,1,1024,256]{3,2,1,0:T(8,128)(2,1)} %get-tuple-element.3, bf16[8,1,1024,256]{3,2,1,0:T(8,128)(2,1)S(1)} %get-tuple-element.2), kind=kLoop, calls=%fused_computation | loop fusion | flops 4194304 | bytes 16777216 | tf_op jit(solution)/shard_map/stack | solution.py:57
  88.8 54.8 %all-to-all-done.1.got_ref = bf16[32,6,2,32,128]{4,3,2,1,0:T(8,128)(2,1)} async-done(((bf16[32,6,2,32,128]{4,3,2,1,0:T(8,128)(2,1)}), bf16[32,6,2,32,128]{4,3,2,1,0:T(8,128)(2,1)}, u32[]{:S(2)}, u32[]{:S(2)}) %all-to-all-start.1) | async-done | bytes 3145760 | tf_op jit(solution)/shard_map/all_to_all | solution.py:337
  143.6 23.2 %grid_step.1 = bf16[32,6,2,32,128]{4,3,2,1,0:T(8,128)(2,1)} custom-call(bf16[32,6,2,32,128]{4,3,2,1,0:T(8,128)(2,1)} %all-to-all-done.1.got_ref, bf16[8,2048,256]{2,1,0:T(8,128)(2,1)} %bitcast.14, bf16[8,2048,256]{2,1,0:T(8,128)(2,1)} %bitcast.15), custom_call_target="tpu_custom_call" | custom-call | flops 12884901888 | bytes 23068672 | tf_op jit(solution)/shard_map/grid_step/pallas_call | solution.py:241
  166.8 0.0 copy-start.1
  166.8 5.4 %all-to-all-start.2 = ((bf16[32,6,2,32,128]{4,3,2,1,0:T(8,128)(2,1)}), bf16[32,6,2,32,128]{4,3,2,1,0:T(8,128)(2,1)}, u32[]{:S(2)}, u32[]{:S(2)}) async-start(bf16[32,6,2,32,128]{4,3,2,1,0:T(8,128)(2,1)} %grid_step.1), calls=%async_computation.2 | async-start | bytes 6291456 | tf_op jit(solution)/shard_map/all_to_all | solution.py:341
  172.8 0.0 copy-done.1
  172.8 2.5 %copy.8 = bf16[4,2,128,8,128]{4,3,2,1,0:T(8,128)(2,1)} copy(bf16[4,2,128,8,128]{2,4,1,0,3:T(8,128)(2,1)S(1)} %bitcast.13) | data formatting | bytes 4194304 | tf_op jit(solution)/shard_map/transpose | solution.py:338
  175.4 4.2 %reshape.308.listed_ref = bf16[4,2,128,1024]{3,2,1,0:T(8,128)(2,1)} reshape(bf16[4,2,128,8,128]{4,3,2,1,0:T(8,128)(2,1)} %copy.8) | data formatting | bytes 4194304 | tf_op jit(solution)/shard_map/reshape | solution.py:339
  179.6 63.8 %all-to-all-done.2.back_ref = bf16[32,6,2,32,128]{4,3,2,1,0:T(8,128)(2,1)} async-done(((bf16[32,6,2,32,128]{4,3,2,1,0:T(8,128)(2,1)}), bf16[32,6,2,32,128]{4,3,2,1,0:T(8,128)(2,1)}, u32[]{:S(2)}, u32[]{:S(2)}) %all-to-all-start.2) | async-done | bytes 3145760 | tf_op jit(solution)/shard_map/all_to_all | solution.py:341
  243.3 9.2 %results.1 = (f32[2,1,2,128,1024]{4,3,2,1,0:T(8,128)}, f32[4,1,2,128,1024]{4,3,2,1,0:T(8,128)}) custom-call(f32[1]{0:T(128)S(6)} %copy.11.step_ref, s32[128,1]{1,0:T(8,128)} %copy.9.waves_ref, bf16[1024,1024]{1,0:T(8,128)(2,1)} %bitcast.12, bf16[32,6,2,32,128]{4,3,2,1,0:T(8,128)(2,1)} %all-to-all-done.2.back_ref, bf16[4,2,128,1024]{3,2,1,0:T(8,128)(2,1)} %reshape.308.listed_ref), custom_call_target="tpu_custom_call" | custom-call | flops 3221225472 | bytes 9437184 | tf_op jit(solution)/shard_map/results/pallas_call | solution.py:304
  (3 shorter events, 0.0 us)
Async XLA Ops:
  0.6 11.7 %copy-start.2 = (s32[1024]{0:T(1024)S(1)}, s32[1024]{0:T(1024)}, u32[]{:S(2)}) copy-start(s32[1024]{0:T(1024)} %param.7) | copy-start | bytes 12292
  6.0 55.4 %all-to-all-start = ((bf16[8,4,2,128,128]{4,3,2,1,0:T(8,128)(2,1)}), bf16[8,4,2,128,128]{4,3,2,1,0:T(8,128)(2,1)S(1)}, u32[]{:S(2)}, u32[]{:S(2)}) async-start(bf16[8,4,2,128,128]{4,3,2,1,0:T(8,128)(2,1)} %permute.1), calls=%async_computation | async-start | bytes 4194304 | tf_op jit(solution)/shard_map/all_to_all | solution.py:332
  61.4 1.3 copy-start
  68.8 74.8 %all-to-all-start.1 = ((bf16[32,6,2,32,128]{4,3,2,1,0:T(8,128)(2,1)}), bf16[32,6,2,32,128]{4,3,2,1,0:T(8,128)(2,1)}, u32[]{:S(2)}, u32[]{:S(2)}) async-start(bf16[32,6,2,32,128]{4,3,2,1,0:T(8,128)(2,1)} %forward_rows.1), calls=%async_computation.1 | async-start | bytes 6291456 | tf_op jit(solution)/shard_map/all_to_all | solution.py:337
  166.8 6.0 %copy-start.1 = (bf16[8,4,2,128,128]{4,3,2,1,0:T(8,128)(2,1)S(1)}, bf16[8,4,2,128,128]{4,3,2,1,0:T(8,128)(2,1)}, u32[]{:S(2)}) copy-start(bf16[8,4,2,128,128]{4,3,2,1,0:T(8,128)(2,1)} %copy-done) | copy-start | bytes 6291460
  166.8 76.5 %all-to-all-start.2 = ((bf16[32,6,2,32,128]{4,3,2,1,0:T(8,128)(2,1)}), bf16[32,6,2,32,128]{4,3,2,1,0:T(8,128)(2,1)}, u32[]{:S(2)}, u32[]{:S(2)}) async-start(bf16[32,6,2,32,128]{4,3,2,1,0:T(8,128)(2,1)} %grid_step.1), calls=%async_computation.2 | async-start | bytes 6291456 | tf_op jit(solution)/shard_map/all_to_all | solution.py:341
